TPU v7x, 32 devices: a whole 2x2x4 slice. The times are simulated.
32 devices in a mesh: tp: 4 (over y, x), grp: 8 (over z, core).
Axes of the slice: x: 2, y: 2, z: 4, core: 2. Of those that a mesh axis runs over, the one named last changes fastest.
Arguments:
- embeds: bfloat16 [2, 32, 8192], P(None, 'grp'), may hold values from -6 to 6
- ssm_state: bfloat16 [2, 32, 128, 64, 128], P(None, 'grp', 'tp'), may hold values from -2 to 2
- conv_state: bfloat16 [2, 32, 3, 8192], P(None, 'grp', None, 'tp'), may hold values from -6 to 6
- norm_gain: float32 [2, 8192], replicated, may hold values from 0.25 to 1.75
- in_weight: bfloat16 [2, 8192, 2, 8192], P(None, 'grp', None, 'tp'), may hold values from -0.0625 to 0.0625
- group_weight: bfloat16 [2, 8192, 384], P(None, 'grp'), may hold values from -0.03125 to 0.03125
- dt_bias: float32 [2, 128], P(None, 'tp'), may hold values from -2 to 1
- a_log: float32 [2, 128], P(None, 'tp'), may hold values from -1.5 to 1.5
- skip_gain: float32 [2, 128], P(None, 'tp'), may hold values from 0.5 to 1.5
- conv_weight: float32 [2, 4, 8192], P(None, None, 'tp'), may hold values from -3 to 3
- conv_bias: float32 [2, 8192], P(None, 'tp'), may hold values from -2 to 2
- out_weight: bfloat16 [2, 8192, 8192], P(None, 'tp', 'grp'), may hold values from -0.0625 to 0.0625
- leave_row: int32 [8], P('grp'), may hold values from 0 to 3
- arrive_from: int32 [8], P('grp'), may hold values from 0 to 7, as said below
Outputs:
- out_hidden: bfloat16 [2, 32, 8192], P(None, 'grp', 'tp')
Inputs may be any that keep to these rules, and one draw needn't show every extreme that they name: Every group appears exactly once in arrive_from: each group's leaving row fills exactly one freed slot.
All inputs are finite; a program needn't handle non-finite values.
Results may differ from a plain program's by a relative error of at most 0.02.
Values may be sent and summed in bfloat16 or wider, within the bound.
A program may use at most 128 MiB of HBM per device.

v0:
```python
import jax
import jax.numpy as jnp
from jax import lax
from jax.sharding import PartitionSpec as P


def local(
    embeds,
    ssm_state,
    conv_state,
    norm_gain,
    in_weight,
    group_weight,
    dt_bias,
    a_log,
    skip_gain,
    conv_weight,
    conv_bias,
    out_weight,
    leave_row,
    arrive_from,
):
    groups = lax.axis_size("grp")
    parts = lax.axis_size("tp")
    part_index = lax.axis_index("tp")
    steps = embeds.shape[0]
    row_dev = embeds.shape[1]
    model_width = embeds.shape[2]
    block_width = model_width // groups
    part_width = model_width // parts
    layers = ssm_state.shape[0]
    heads_dev = ssm_state.shape[2]
    head_dim = ssm_state.shape[3]
    state_dim = ssm_state.shape[4]
    channels = in_weight.shape[3]
    taps_count = conv_weight.shape[1]
    state_list = [ssm_state[i] for i in range(layers)]
    conv_list = [conv_state[i] for i in range(layers)]
    leaving = leave_row[0]
    anchor = arrive_from[0]

    def pick(carry, piece):
        count = piece[0].shape[0]
        hits = jnp.arange(count, dtype=jnp.int32) == anchor
        picked = []
        for total, member in zip(carry, piece):
            mask = hits.reshape((count,) + (1,) * (member.ndim - 1))
            picked.append(jnp.sum(jnp.where(mask, member, jnp.zeros_like(member)), axis=0))
        return tuple(picked)

    def leaving_rows():
        own_state = jnp.stack(
            [lax.dynamic_index_in_dim(s_arr, leaving, 0, False) for s_arr in state_list]
        )
        own_conv = jnp.stack(
            [lax.dynamic_index_in_dim(c_arr, leaving, 0, False) for c_arr in conv_list]
        )
        return (own_state, own_conv)

    def store_rows(got_state, got_conv):
        for i in range(layers):
            state_list[i] = lax.dynamic_update_index_in_dim(state_list[i], got_state[i], leaving, 0)
            conv_list[i] = lax.dynamic_update_index_in_dim(conv_list[i], got_conv[i], leaving, 0)

    def migrate_all():
        own_state, own_conv = leaving_rows()
        start_pair = (
            jnp.zeros(own_state.shape, jnp.bfloat16),
            jnp.zeros(own_conv.shape, jnp.bfloat16),
        )
        got_state, got_conv = pick(
            start_pair,
            (
                lax.all_gather(own_state[None], "grp", axis=0, tiled=True),
                lax.all_gather(own_conv[None], "grp", axis=0, tiled=True),
            ),
        )
        store_rows(got_state, got_conv)

    def migrate(layer):
        if layer == 0:
            migrate_all()

    def mixer(normed_block, layer):
        w_cols = in_weight[layer].reshape(block_width, 2 * channels)
        w_group = group_weight[layer]
        first = jnp.dot(normed_block, w_cols, preferred_element_type=jnp.float32)
        second = jnp.dot(normed_block, w_group, preferred_element_type=jnp.float32)
        summed = lax.psum_scatter(
            jnp.concatenate([first, second], axis=1), "grp", scatter_dimension=0, tiled=True
        )
        x_part = summed[:, :channels].astype(jnp.bfloat16)
        z_part = summed[:, channels : 2 * channels]
        b_mat = summed[:, 2 * channels : 2 * channels + state_dim]
        c_mat = summed[:, 2 * channels + state_dim : 2 * channels + 2 * state_dim]
        dt_all = summed[:, 2 * channels + 2 * state_dim :]
        dt_raw = lax.dynamic_slice_in_dim(dt_all, part_index * heads_dev, heads_dev, 1)
        taps = conv_weight[layer]
        window = conv_list[layer]
        conv_sum = x_part.astype(jnp.float32) * taps[taps_count - 1] + conv_bias[layer]
        for k in range(taps_count - 1):
            conv_sum = conv_sum + window[:, k].astype(jnp.float32) * taps[k]
        xc = jax.nn.silu(conv_sum)
        conv_list[layer] = jnp.concatenate([window[:, 1:], x_part[:, None, :]], axis=1)
        step_size = jax.nn.softplus(dt_raw + dt_bias[layer])
        decay = jnp.exp(-step_size * jnp.exp(a_log[layer]))
        xh = xc.reshape(row_dev, heads_dev, head_dim)
        fresh = (
            state_list[layer].astype(jnp.float32) * decay[:, :, None, None]
            + (step_size[:, :, None] * xh)[..., None] * b_mat[:, None, None, :]
        )
        state_list[layer] = fresh.astype(jnp.bfloat16)
        out_y = (
            jnp.sum(fresh * c_mat[:, None, None, :], axis=-1) + skip_gain[layer][None, :, None] * xh
        )
        gated = (out_y.reshape(row_dev, channels) * jax.nn.silu(z_part)).astype(jnp.bfloat16)
        w_back = out_weight[layer]
        partial_out = jnp.dot(
            lax.all_gather(gated, "grp", axis=0, tiled=True),
            w_back,
            preferred_element_type=jnp.float32,
        )
        return lax.psum(partial_out, "tp").astype(jnp.bfloat16)

    results = []
    for section in range(steps):
        carried = section > 0
        hidden = embeds[section]
        for layer in range(layers):
            if carried:
                migrate(layer)
            hf = hidden.astype(jnp.float32)
            normed = (
                hf * lax.rsqrt(jnp.mean(hf * hf, axis=-1, keepdims=True) + 1e-05) * norm_gain[layer]
            ).astype(jnp.bfloat16)
            normed_block = lax.all_to_all(normed, "grp", split_axis=1, concat_axis=0, tiled=True)
            delta = mixer(normed_block, layer)
            delta_rows = lax.all_to_all(delta, "grp", split_axis=0, concat_axis=1, tiled=True)
            hidden = (hf + delta_rows.astype(jnp.float32)).astype(jnp.bfloat16)
        results.append(lax.dynamic_slice_in_dim(hidden, part_index * part_width, part_width, 1))
    return jnp.stack(results)


def solution(mesh):
    placed = (
        P(None, "grp", None),
        P(None, "grp", "tp", None, None),
        P(None, "grp", None, "tp"),
        P(),
        P(None, "grp", None, "tp"),
        P(None, "grp", None),
        P(None, "tp"),
        P(None, "tp"),
        P(None, "tp"),
        P(None, None, "tp"),
        P(None, "tp"),
        P(None, "tp", "grp"),
        P("grp"),
        P("grp"),
    )
    return jax.shard_map(
        local, mesh=mesh, in_specs=placed, out_specs=P(None, "grp", "tp"), check_vma=False
    )
```

profile of v0, /device:TPU:0, one launch (start us, length us, event | category | flops | bytes accessed | tf_op | source)
XLA Modules:
  0.0 559.2 jit_solution(1863969251240788435)
XLA Ops:
  10.4 6.4 %all-to-all-start.4 = ((bf16[4,8,1024]{2,0,1:T(4,128)(2,1)}), bf16[4,8,1024]{2,0,1:T(4,128)(2,1)S(1)}, u32[]{:S(2)}, u32[]{:S(2)}) async-start(bf16[4,8,1024]{2,0,1:T(4,128)(2,1)} %get-tuple-element.60), calls=%async_computation.4 | async-start | bytes 131072 | tf_op jit(solution)/shard_map/all_to_all | solution.py:136
  16.8 14.3 %fusion.74 = (bf16[1,1024,2,2048]{3,2,1,0:T(2,128)(2,1)}, bf16[1,1024,2,2048]{3,2,1,0:T(2,128)(2,1)}) fusion(bf16[2,1024,2,2048]{3,2,1,0:T(2,128)(2,1)} %param.18), kind=kLoop, calls=%fused_computation.180 | loop fusion | bytes 33554432 | tf_op jit(solution)/shard_map/slice | solution.py:85
  31.1 12.1 %copy.33 = bf16[128,8,2,2048]{3,1,2,0:T(8,128)(2,1)} copy(bf16[128,8,2,2048]{3,2,1,0:T(2,128)(2,1)} %bitcast.216) | data formatting | bytes 16777216
  44.1 12.2 %copy.34 = bf16[128,8,2,2048]{3,1,2,0:T(8,128)(2,1)} copy(bf16[128,8,2,2048]{3,2,1,0:T(2,128)(2,1)} %bitcast.215) | data formatting | bytes 16777216
  57.5 5.1 all-to-all-start
  63.5 5.1 all-to-all-done
  68.8 4.9 fusion.82
  74.6 4.9 fusion.84
  79.5 50.4 %all-reduce.13.cloned.1.call-done = f32[32,4480]{1,0:T(8,128)} async-done(((f32[32,4480]{1,0:T(8,128)}), f32[32,4480]{1,0:T(8,128)}) %all-reduce.13.cloned.1.call-update) | async-done | bytes 573456
  132.0 4.2 fusion.11
  137.3 14.0 %all-gather.2 = bf16[8,4,2048]{2,1,0:T(4,128)(2,1)S(1)} all-gather(bf16[1,4,2048]{2,1,0:T(4,128)(2,1)S(1)} %fusion.62), channel_id=1, replica_groups=mesh['tp'=4,'grp'=8] {'grp'}, dimensions={0}, use_global_device_ids=true | all-gather | bytes 147456 | tf_op jit(solution)/shard_map/all_gather | solution.py:119
  155.1 18.5 %all-reduce.18 = bf16[32,1024]{1,0:T(8,128)(2,1)S(1)} all-reduce(f32[32,1024]{1,0:T(8,128)S(1)} %fusion.8), channel_id=1, replica_groups=mesh['tp'=4,'grp'=8] {'tp'}, use_global_device_ids=true, to_apply=%region_3.4 | all-reduce | flops 32768 | bytes 196608 | tf_op jit(solution)/shard_map/psum | solution.py:123
  179.0 4.5 all-to-all-done.1
  188.7 4.9 all-to-all-done.2
  195.0 4.9 fusion.83
  201.6 55.8 %all-reduce.17.cloned.1.call-done = (f32[32,4480]{1,0:T(8,128)}, f32[32,4480]{1,0:T(8,128)}) async-done(((f32[32,4480]{1,0:T(8,128)}, f32[32,4480]{1,0:T(8,128)}), (f32[32,4480]{1,0:T(8,128)}, f32[32,4480]{1,0:T(8,128)})) %all-reduce.17.cloned.1.call-update) | async-done | bytes 1146896
  259.4 4.2 multiply_reduce_fusion.2
  268.8 15.4 %all-gather.1 = bf16[16,3,2048]{2,1,0:T(4,128)(2,1)S(1)} all-gather(bf16[2,3,2048]{2,1,0:T(4,128)(2,1)S(1)} %copy.29), channel_id=3, replica_groups=mesh['tp'=4,'grp'=8] {'grp'}, dimensions={0}, use_global_device_ids=true | all-gather | bytes 221184 | tf_op jit(solution)/shard_map/all_gather | solution.py:75
  286.8 61.5 %all-gather.8.cloned.1.call-done = bf16[16,32,64,128]{3,2,1,0:T(8,128)(2,1)} async-done(((bf16[2,32,64,128]{3,2,1,0:T(8,128)(2,1)}), bf16[16,32,64,128]{3,2,1,0:T(8,128)(2,1)}) %all-gather.8.cloned.1.call-update) | async-done | bytes 8388624 | tf_op jit(solution)/shard_map/all_gather | solution.py:74
  348.3 5.6 select_reduce_fusion
  358.9 14.0 %all-gather.4 = bf16[8,4,2048]{2,1,0:T(4,128)(2,1)S(1)} all-gather(bf16[1,4,2048]{2,1,0:T(4,128)(2,1)S(1)} %fusion.64), channel_id=1, replica_groups=mesh['tp'=4,'grp'=8] {'grp'}, dimensions={0}, use_global_device_ids=true | all-gather | bytes 147456 | tf_op jit(solution)/shard_map/all_gather | solution.py:119
  375.9 18.5 %all-reduce.19 = bf16[32,1024]{1,0:T(8,128)(2,1)S(1)} all-reduce(f32[32,1024]{1,0:T(8,128)S(1)} %fusion.6), channel_id=1, replica_groups=mesh['tp'=4,'grp'=8] {'tp'}, use_global_device_ids=true, to_apply=%region_13.14 | all-reduce | flops 32768 | bytes 196608 | tf_op jit(solution)/shard_map/psum | solution.py:123
  394.4 8.3 %all_to_all.116 = bf16[8,4,1024]{2,1,0:T(4,128)(2,1)S(1)} all-to-all(bf16[8,4,1024]{2,1,0:T(4,128)(2,1)S(1)} %all_to_all.101), channel_id=1, replica_groups=mesh['tp'=4,'grp'=8] {'grp'}, dimensions={0} | all-to-all | bytes 131072 | tf_op jit(solution)/shard_map/all_to_all | solution.py:138
  403.0 8.3 %all_to_all.117 = bf16[4,8,1024]{2,0,1:T(4,128)(2,1)S(1)} all-to-all(bf16[4,8,1024]{2,0,1:T(4,128)(2,1)S(1)} %multiply_convert_fusion), channel_id=1, replica_groups=mesh['tp'=4,'grp'=8] {'grp'}, dimensions={1} | all-to-all | bytes 131072 | tf_op jit(solution)/shard_map/all_to_all | solution.py:136
  411.6 5.1 fusion.85
  418.1 53.1 %all-reduce.15.cloned.1.call-done = f32[32,4480]{1,0:T(8,128)} async-done(((f32[32,4480]{1,0:T(8,128)}), f32[32,4480]{1,0:T(8,128)}) %all-reduce.15.cloned.1.call-update) | async-done | bytes 573456
  477.2 14.0 %all-gather.5 = bf16[8,4,2048]{2,1,0:T(4,128)(2,1)S(1)} all-gather(bf16[1,4,2048]{2,1,0:T(4,128)(2,1)S(1)} %get-tuple-element.64), channel_id=1, replica_groups=mesh['tp'=4,'grp'=8] {'grp'}, dimensions={0}, use_global_device_ids=true | all-gather | bytes 147456 | tf_op jit(solution)/shard_map/all_gather | solution.py:119
  494.3 14.0 %all-gather.3 = bf16[8,4,2048]{2,1,0:T(4,128)(2,1)S(1)} all-gather(bf16[1,4,2048]{2,1,0:T(4,128)(2,1)S(1)} %get-tuple-element.63), channel_id=1, replica_groups=mesh['tp'=4,'grp'=8] {'grp'}, dimensions={0}, use_global_device_ids=true | all-gather | bytes 147456 | tf_op jit(solution)/shard_map/all_gather | solution.py:119
  511.3 21.7 %all-reduce.20 = (bf16[32,1024]{1,0:T(8,128)(2,1)S(1)}, bf16[32,1024]{1,0:T(8,128)(2,1)S(1)}) all-reduce(f32[32,1024]{1,0:T(8,128)S(1)} %fusion.2, f32[32,1024]{1,0:T(8,128)S(1)} %fusion.4), channel_id=1, replica_groups=mesh['tp'=4,'grp'=8] {'tp'}, use_global_device_ids=true, to_apply=%region_17.18 | all-reduce | flops 65536 | bytes 393216 | tf_op jit(solution)/shard_map/psum | solution.py:123
  537.6 5.2 all-to-all-done.7
  542.8 3.3 all-to-all-start.3
  546.2 5.8 %all-to-all-done.3 = bf16[8,4,1024]{2,1,0:T(4,128)(2,1)S(1)} async-done(((bf16[8,4,1024]{2,1,0:T(4,128)(2,1)}), bf16[8,4,1024]{2,1,0:T(4,128)(2,1)S(1)}, u32[]{:S(2)}, u32[]{:S(2)}) %all-to-all-start.3) | async-done | bytes 65568 | tf_op jit(solution)/shard_map/all_to_all | solution.py:138
  (162 shorter events, 63.6 us)
Async XLA Ops:
  10.4 47.1 %all-to-all-start.4 = ((bf16[4,8,1024]{2,0,1:T(4,128)(2,1)}), bf16[4,8,1024]{2,0,1:T(4,128)(2,1)S(1)}, u32[]{:S(2)}, u32[]{:S(2)}) async-start(bf16[4,8,1024]{2,0,1:T(4,128)(2,1)} %get-tuple-element.60), calls=%async_computation.4 | async-start | bytes 131072 | tf_op jit(solution)/shard_map/all_to_all | solution.py:136
  31.0 12.1 %copy-start.5 = (bf16[2,4,3,2048]{3,1,2,0:T(4,128)(2,1)S(1)}, bf16[2,4,3,2048]{3,1,2,0:T(4,128)(2,1)}, u32[]{:S(2)}) copy-start(bf16[2,4,3,2048]{3,1,2,0:T(4,128)(2,1)} %param.16) | copy-start | bytes 294916
  31.1 12.2 %copy-start.8 = (f32[2,4,2048]{2,1,0:T(4,128)S(1)}, f32[2,4,2048]{2,1,0:T(4,128)}, u32[]{:S(2)}) copy-start(f32[2,4,2048]{2,1,0:T(4,128)} %param.23) | copy-start | bytes 196612
  31.1 12.2 %copy-start.9 = (f32[2,2048]{1,0:T(2,128)S(1)}, f32[2,2048]{1,0:T(2,128)}, u32[]{:S(2)}) copy-start(f32[2,2048]{1,0:T(2,128)} %param.24) | copy-start | bytes 49156
  31.1 12.3 %copy-start.19 = (f32[2,32]{1,0:T(2,128)S(1)}, f32[2,32]{1,0:T(2,128)}, u32[]{:S(2)}) copy-start(f32[2,32]{1,0:T(2,128)} %param.22) | copy-start | bytes 772
  44.1 92.3 %copy-start.6 = (f32[2048]{0:T(1024)}, f32[2048]{0:T(1024)S(1)}, u32[]{:S(2)}) copy-start(f32[2048]{0:T(1024)S(1)} %mul.533) | copy-start | bytes 24580
  44.1 12.2 %copy-start.22 = (u32[32]{0:T(128)S(1)}, u32[32]{0:T(128)}, u32[]{:S(2)}) copy-start(u32[32]{0:T(128)} %constant.77) | copy-start | bytes 388
  44.1 18.8 %copy-start.20 = (f32[2,32]{1,0:T(2,128)S(1)}, f32[2,32]{1,0:T(2,128)}, u32[]{:S(2)}) copy-start(f32[2,32]{1,0:T(2,128)} %param.21) | copy-start | bytes 772
  44.1 18.8 %copy-start.21 = (f32[2,32]{1,0:T(2,128)S(1)}, f32[2,32]{1,0:T(2,128)}, u32[]{:S(2)}) copy-start(f32[2,32]{1,0:T(2,128)} %param.20) | copy-start | bytes 772
  44.1 24.5 %copy-start.2 = (bf16[2,1024,384]{2,1,0:T(8,128)(2,1)S(1)}, bf16[2,1024,384]{2,1,0:T(8,128)(2,1)}, u32[]{:S(2)}) copy-start(bf16[2,1024,384]{2,1,0:T(8,128)(2,1)} %param.19) | copy-start | bytes 4718596
  57.5 11.0 %all-to-all-start = ((bf16[4,8,1024]{2,0,1:T(4,128)(2,1)}), bf16[4,8,1024]{2,0,1:T(4,128)(2,1)S(1)}, u32[]{:S(2)}, u32[]{:S(2)}) async-start(bf16[4,8,1024]{2,0,1:T(4,128)(2,1)} %get-tuple-element.59), calls=%async_computation | async-start | bytes 131072 | tf_op jit(solution)/shard_map/all_to_all | solution.py:136
  62.6 67.3 %all-reduce.13.cloned.1.call-start = ((), (), s32[]{:S(2)}) async-start(), calls=%async_computation.9 | async-start | bytes 1146880
  63.5 68.4 %copy-start.14 = (f32[32]{0:T(128)}, f32[32]{0:T(128)S(1)}, u32[]{:S(2)}) copy-start(f32[32]{0:T(128)S(1)} %get-tuple-element.70) | copy-start | bytes 388
  63.5 68.4 %copy-start.16 = (f32[32]{0:T(128)}, f32[32]{0:T(128)S(1)}, u32[]{:S(2)}) copy-start(f32[32]{0:T(128)S(1)} %get-tuple-element.73) | copy-start | bytes 388
  136.2 47.2 %copy-start.4 = (bf16[2,4,8192]{2,1,0:T(4,128)(2,1)S(1)}, bf16[2,4,8192]{2,1,0:T(4,128)(2,1)}, u32[]{:S(2)}) copy-start(bf16[2,4,8192]{2,1,0:T(4,128)(2,1)} %param.14) | copy-start | bytes 393220
  174.2 9.2 %all-to-all-start.1 = ((bf16[8,4,1024]{2,1,0:T(4,128)(2,1)}), bf16[8,4,1024]{2,1,0:T(4,128)(2,1)S(1)}, u32[]{:S(2)}, u32[]{:S(2)}) async-start(bf16[8,4,1024]{2,1,0:T(4,128)(2,1)} %all_to_all.91), calls=%async_computation.1 | async-start | bytes 131072 | tf_op jit(solution)/shard_map/all_to_all | solution.py:138
  184.4 9.2 %all-to-all-start.2 = ((bf16[4,8,1024]{2,0,1:T(4,128)(2,1)}), bf16[4,8,1024]{2,0,1:T(4,128)(2,1)S(1)}, u32[]{:S(2)}, u32[]{:S(2)}) async-start(bf16[4,8,1024]{2,0,1:T(4,128)(2,1)} %multiply_convert_fusion.2), calls=%async_computation.2 | async-start | bytes 131072 | tf_op jit(solution)/shard_map/all_to_all | solution.py:136
  187.8 69.6 %all-reduce.17.cloned.1.call-start = ((), (), s32[]{:S(2)}) async-start(), calls=%async_computation.11 | async-start | bytes 2293760
  195.0 64.2 %copy-start.10 = (f32[32]{0:T(128)S(1)}, f32[32]{0:T(128)}, u32[]{:S(2)}) copy-start(f32[32]{0:T(128)} %get-tuple-element.69) | copy-start | bytes 388
  195.0 64.2 %copy-start.12 = (f32[32]{0:T(128)S(1)}, f32[32]{0:T(128)}, u32[]{:S(2)}) copy-start(f32[32]{0:T(128)} %get-tuple-element.74) | copy-start | bytes 388
  200.8 147.5 %all-gather.8.cloned.1.call-start = ((), (), s32[]{:S(2)}) async-start(), calls=%async_computation.8 | async-start | bytes 9437184 | tf_op jit(solution)/shard_map/all_gather | solution.py:74
  259.4 27.2 %copy-start.15 = (f32[32]{0:T(128)S(1)}, f32[32]{0:T(128)}, u32[]{:S(2)}) copy-start(f32[32]{0:T(128)} %copy-done.14) | copy-start | bytes 388
  259.4 27.2 %copy-start.17 = (f32[32]{0:T(128)S(1)}, f32[32]{0:T(128)}, u32[]{:S(2)}) copy-start(f32[32]{0:T(128)} %copy-done.16) | copy-start | bytes 388
  266.1 205.1 %all-reduce.15.cloned.1.call-start = ((), (), s32[]{:S(2)}) async-start(), calls=%async_computation.10 | async-start | bytes 1146880
  353.9 3.8 copy-start.7
  357.7 53.7 %copy-start.3 = (bf16[2,1024,384]{2,1,0:T(8,128)(2,1)S(1)}, bf16[2,1024,384]{2,1,0:T(8,128)(2,1)}, u32[]{:S(2)}) copy-start(bf16[2,1024,384]{2,1,0:T(8,128)(2,1)} %param.19) | copy-start | bytes 4718596
  411.6 6.0 %copy-start.18 = (f32[32]{0:T(128)S(1)}, f32[32]{0:T(128)}, u32[]{:S(2)}) copy-start(f32[32]{0:T(128)} %get-tuple-element.65) | copy-start | bytes 388
  411.6 61.4 %copy-start.11 = (f32[32]{0:T(128)S(1)}, f32[32]{0:T(128)}, u32[]{:S(2)}) copy-start(f32[32]{0:T(128)} %get-tuple-element.69) | copy-start | bytes 388
  411.6 61.4 %copy-start.13 = (f32[32]{0:T(128)S(1)}, f32[32]{0:T(128)}, u32[]{:S(2)}) copy-start(f32[32]{0:T(128)} %get-tuple-element.74) | copy-start | bytes 388
  411.6 61.6 %copy-start.1 = (bf16[4,32,64,128]{3,2,1,0:T(8,128)(2,1)S(1)}, bf16[4,32,64,128]{3,2,1,0:T(8,128)(2,1)}, u32[]{:S(2)}) copy-start(bf16[4,32,64,128]{3,2,1,0:T(8,128)(2,1)} %get-tuple-element.31) | copy-start | bytes 6291460
  533.6 9.2 %all-to-all-start.7 = ((bf16[8,4,1024]{2,1,0:T(4,128)(2,1)}), bf16[8,4,1024]{2,1,0:T(4,128)(2,1)S(1)}, u32[]{:S(2)}, u32[]{:S(2)}) async-start(bf16[8,4,1024]{2,1,0:T(4,128)(2,1)} %all_to_all.106), calls=%async_computation.7 | async-start | bytes 131072 | tf_op jit(solution)/shard_map/all_to_all | solution.py:138
  542.8 9.2 %all-to-all-start.3 = ((bf16[8,4,1024]{2,1,0:T(4,128)(2,1)}), bf16[8,4,1024]{2,1,0:T(4,128)(2,1)S(1)}, u32[]{:S(2)}, u32[]{:S(2)}) async-start(bf16[8,4,1024]{2,1,0:T(4,128)(2,1)} %all_to_all.96), calls=%async_computation.3 | async-start | bytes 131072 | tf_op jit(solution)/shard_map/all_to_all | solution.py:138
  (1 other events, 1.3 us)
Sparse Core Ops, SparseCore 0:
  74.7 55.1 all-reduce.12
  200.9 56.3 all-reduce.16
  266.2 82.0 all-gather.7
  417.7 53.4 all-reduce.14
where the time goes:
time: 561 us; the launch traced here: 559 us
  waiting for transfers between devices  246 us (44%)
  blocking collectives  146 us (26%)
  local copies, waits for them, and re-layouts  53.6 us (10%)
  other arithmetic  36.8 us (7%)
  matrix products  35.1 us (6%)
  starting transfers between devices  25.2 us (4%)
  between operations  15.8 us (3%)
    unnamed x7, waiting for transfers between devices  159 us
    all_gather x1, waiting for transfers between devices, migrate_all(): lax.all_gather(own_state[None], 'grp', axis=0, tiled=True)  61.5 us
    psum x3, blocking collectives, mixer(): return lax.psum(partial_out, 'tp').astype(jnp.bfloat16)  58.6 us
    all_gather x4, blocking collectives, mixer(): lax.all_gather(gated, 'grp', axis=0, tiled=True)  55.9 us
    unnamed x53, local copies, waits for them, and re-layouts  27 us
    dot_general x4, matrix products, mixer(): first = jnp.dot(normed_block, w_cols, preferred_element_type=jnp.float32)  19.9 us
    all_to_all x3, waiting for transfers between devices, local(): lax.all_to_all(delta, 'grp', split_axis=0, concat_axis=1, tiled=True)  15.5 us
    all_gather x1, blocking collectives, migrate_all(): lax.all_gather(own_conv[None], 'grp', axis=0, tiled=True)  15.4 us
  transfers between devices with their start and end apart: 10, of which 9 were waited for; matrix products, arithmetic and copies ran while one was open for 9% of the time, Pallas kernels for 0%

commit v1 on v0

--- a/solution.py
+++ b/solution.py
@@ -135,7 +135,12 @@
             ).astype(jnp.bfloat16)
             normed_block = lax.all_to_all(normed, "grp", split_axis=1, concat_axis=0, tiled=True)
             delta = mixer(normed_block, layer)
-            delta_rows = lax.all_to_all(delta, "grp", split_axis=0, concat_axis=1, tiled=True)
+            delta_rows = jnp.concatenate(
+                lax.all_to_all(
+                    jnp.stack(jnp.split(delta, lax.axis_size("grp"), axis=0)), "grp", 0, 0
+                ),
+                axis=1,
+            )
             hidden = (hf + delta_rows.astype(jnp.float32)).astype(jnp.bfloat16)
         results.append(lax.dynamic_slice_in_dim(hidden, part_index * part_width, part_width, 1))
     return jnp.stack(results)

time: 561 us -> 570 us (1.016)
  local copies, waits for them, and re-layouts: 53.6 us -> 66.1 us
    unnamed x53 -> x81, local copies, waits for them, and re-layouts: 27 us -> 39.7 us
  transfers between devices with their start and end apart: 10 -> 10, of which waited for: 9 -> 9; matrix products, arithmetic and copies ran while one was open for 9% -> 10% of each run, Pallas kernels for 0% -> 0%
where the time goes in v1:
time: 570 us; the launch traced here: 568 us
  waiting for transfers between devices  242 us (42%)
  blocking collectives  146 us (26%)
  local copies, waits for them, and re-layouts  66.1 us (12%)
  other arithmetic  36.8 us (6%)
  matrix products  35.1 us (6%)
  starting transfers between devices  25.8 us (5%)
  between operations  15.8 us (3%)
    unnamed x7, waiting for transfers between devices  159 us
    all_gather x1, waiting for transfers between devices, migrate_all(): lax.all_gather(own_state[None], 'grp', axis=0, tiled=True)  61.5 us
    psum x3, blocking collectives, mixer(): return lax.psum(partial_out, 'tp').astype(jnp.bfloat16)  58.6 us
    all_gather x4, blocking collectives, mixer(): lax.all_gather(gated, 'grp', axis=0, tiled=True)  55.9 us
    unnamed x81, local copies, waits for them, and re-layouts  39.7 us
    dot_general x4, matrix products, mixer(): first = jnp.dot(normed_block, w_cols, preferred_element_type=jnp.float32)  19.9 us
    all_gather x1, blocking collectives, migrate_all(): lax.all_gather(own_conv[None], 'grp', axis=0, tiled=True)  15.4 us
    all_to_all x3, starting transfers between devices, local(): lax.all_to_all(normed, 'grp', split_axis=1, concat_axis=0, tiled=True)  14.8 us
  transfers between devices with their start and end apart: 10, of which 9 were waited for; matrix products, arithmetic and copies ran while one was open for 10% of the time, Pallas kernels for 0%

profile of v1, /device:TPU:0, one launch (start us, length us, event | category | flops | bytes accessed | tf_op | source)
XLA Modules:
  0.0 568.3 jit_solution(8583019725025389359)
XLA Ops:
  10.4 6.4 %all-to-all-start.4 = ((bf16[4,8,1024]{2,0,1:T(4,128)(2,1)}), bf16[4,8,1024]{2,0,1:T(4,128)(2,1)S(1)}, u32[]{:S(2)}, u32[]{:S(2)}) async-start(bf16[4,8,1024]{2,0,1:T(4,128)(2,1)} %get-tuple-element.60), calls=%async_computation.4 | async-start | bytes 131072 | tf_op jit(solution)/shard_map/all_to_all | solution.py:136
  16.8 14.3 %fusion.74 = (bf16[1,1024,2,2048]{3,2,1,0:T(2,128)(2,1)}, bf16[1,1024,2,2048]{3,2,1,0:T(2,128)(2,1)}) fusion(bf16[2,1024,2,2048]{3,2,1,0:T(2,128)(2,1)} %param.18), kind=kLoop, calls=%fused_computation.244 | loop fusion | bytes 33554432 | tf_op jit(solution)/shard_map/slice | solution.py:85
  31.1 12.1 %copy.19 = bf16[128,8,2,2048]{3,1,2,0:T(8,128)(2,1)} copy(bf16[128,8,2,2048]{3,2,1,0:T(2,128)(2,1)} %bitcast.342) | data formatting | bytes 16777216
  44.1 12.2 %copy.20 = bf16[128,8,2,2048]{3,1,2,0:T(8,128)(2,1)} copy(bf16[128,8,2,2048]{3,2,1,0:T(2,128)(2,1)} %bitcast.341) | data formatting | bytes 16777216
  57.5 5.1 all-to-all-start
  63.5 5.1 all-to-all-done
  68.8 4.9 fusion.82
  74.6 4.9 fusion.84
  79.5 50.4 %all-reduce.13.cloned.1.call-done = f32[32,4480]{1,0:T(8,128)} async-done(((f32[32,4480]{1,0:T(8,128)}), f32[32,4480]{1,0:T(8,128)}) %all-reduce.13.cloned.1.call-update) | async-done | bytes 573456
  132.0 4.2 fusion.11
  137.3 14.0 %all-gather.2 = bf16[8,4,2048]{2,1,0:T(4,128)(2,1)S(1)} all-gather(bf16[1,4,2048]{2,1,0:T(4,128)(2,1)S(1)} %fusion.62), channel_id=1, replica_groups=mesh['tp'=4,'grp'=8] {'grp'}, dimensions={0}, use_global_device_ids=true | all-gather | bytes 147456 | tf_op jit(solution)/shard_map/all_gather | solution.py:119
  155.1 18.5 %all-reduce.18 = bf16[32,1024]{1,0:T(8,128)(2,1)S(1)} all-reduce(f32[32,1024]{1,0:T(8,128)S(1)} %fusion.8), channel_id=1, replica_groups=mesh['tp'=4,'grp'=8] {'tp'}, use_global_device_ids=true, to_apply=%region_3.4 | all-reduce | flops 32768 | bytes 196608 | tf_op jit(solution)/shard_map/psum | solution.py:123
  178.4 3.3 all-to-all-start.1
  183.1 4.5 all-to-all-done.1
  192.8 4.9 all-to-all-done.2
  199.1 4.9 fusion.83
  205.7 55.8 %all-reduce.17.cloned.1.call-done = (f32[32,4480]{1,0:T(8,128)}, f32[32,4480]{1,0:T(8,128)}) async-done(((f32[32,4480]{1,0:T(8,128)}, f32[32,4480]{1,0:T(8,128)}), (f32[32,4480]{1,0:T(8,128)}, f32[32,4480]{1,0:T(8,128)})) %all-reduce.17.cloned.1.call-update) | async-done | bytes 1146896
  263.6 4.2 multiply_reduce_fusion.2
  273.0 15.4 %all-gather.1 = bf16[16,3,2048]{2,1,0:T(4,128)(2,1)S(1)} all-gather(bf16[2,3,2048]{2,1,0:T(4,128)(2,1)S(1)} %copy.16), channel_id=3, replica_groups=mesh['tp'=4,'grp'=8] {'grp'}, dimensions={0}, use_global_device_ids=true | all-gather | bytes 221184 | tf_op jit(solution)/shard_map/all_gather | solution.py:75
  291.0 61.5 %all-gather.8.cloned.1.call-done = bf16[16,32,64,128]{3,2,1,0:T(8,128)(2,1)} async-done(((bf16[2,32,64,128]{3,2,1,0:T(8,128)(2,1)}), bf16[16,32,64,128]{3,2,1,0:T(8,128)(2,1)}) %all-gather.8.cloned.1.call-update) | async-done | bytes 8388624 | tf_op jit(solution)/shard_map/all_gather | solution.py:74
  352.5 5.6 select_reduce_fusion
  363.0 14.0 %all-gather.4 = bf16[8,4,2048]{2,1,0:T(4,128)(2,1)S(1)} all-gather(bf16[1,4,2048]{2,1,0:T(4,128)(2,1)S(1)} %fusion.64), channel_id=1, replica_groups=mesh['tp'=4,'grp'=8] {'grp'}, dimensions={0}, use_global_device_ids=true | all-gather | bytes 147456 | tf_op jit(solution)/shard_map/all_gather | solution.py:119
  380.0 18.5 %all-reduce.19 = bf16[32,1024]{1,0:T(8,128)(2,1)S(1)} all-reduce(f32[32,1024]{1,0:T(8,128)S(1)} %fusion.6), channel_id=1, replica_groups=mesh['tp'=4,'grp'=8] {'tp'}, use_global_device_ids=true, to_apply=%region_13.14 | all-reduce | flops 32768 | bytes 196608 | tf_op jit(solution)/shard_map/psum | solution.py:123
  398.7 8.3 %all_to_all.84 = bf16[8,4,1024]{2,1,0:T(4,128)(2,1)S(1)} all-to-all(bf16[8,4,1024]{2,1,0:T(4,128)(2,1)S(1)} %constant_dynamic-update-slice_fusion.16), channel_id=1, replica_groups=mesh['tp'=4,'grp'=8] {'grp'}, dimensions={0} | all-to-all | bytes 131072 | tf_op jit(solution)/shard_map/all_to_all | solution.py:139
  407.3 8.3 %all_to_all.85 = bf16[4,8,1024]{2,0,1:T(4,128)(2,1)S(1)} all-to-all(bf16[4,8,1024]{2,0,1:T(4,128)(2,1)S(1)} %multiply_convert_fusion), channel_id=1, replica_groups=mesh['tp'=4,'grp'=8] {'grp'}, dimensions={1} | all-to-all | bytes 131072 | tf_op jit(solution)/shard_map/all_to_all | solution.py:136
  415.9 5.1 fusion.85
  422.3 53.1 %all-reduce.15.cloned.1.call-done = f32[32,4480]{1,0:T(8,128)} async-done(((f32[32,4480]{1,0:T(8,128)}), f32[32,4480]{1,0:T(8,128)}) %all-reduce.15.cloned.1.call-update) | async-done | bytes 573456
  481.5 14.0 %all-gather.5 = bf16[8,4,2048]{2,1,0:T(4,128)(2,1)S(1)} all-gather(bf16[1,4,2048]{2,1,0:T(4,128)(2,1)S(1)} %get-tuple-element.64), channel_id=1, replica_groups=mesh['tp'=4,'grp'=8] {'grp'}, dimensions={0}, use_global_device_ids=true | all-gather | bytes 147456 | tf_op jit(solution)/shard_map/all_gather | solution.py:119
  498.5 14.0 %all-gather.3 = bf16[8,4,2048]{2,1,0:T(4,128)(2,1)S(1)} all-gather(bf16[1,4,2048]{2,1,0:T(4,128)(2,1)S(1)} %get-tuple-element.63), channel_id=1, replica_groups=mesh['tp'=4,'grp'=8] {'grp'}, dimensions={0}, use_global_device_ids=true | all-gather | bytes 147456 | tf_op jit(solution)/shard_map/all_gather | solution.py:119
  515.5 21.6 %all-reduce.20 = (bf16[32,1024]{1,0:T(8,128)(2,1)S(1)}, bf16[32,1024]{1,0:T(8,128)(2,1)S(1)}) all-reduce(f32[32,1024]{1,0:T(8,128)S(1)} %fusion.2, f32[32,1024]{1,0:T(8,128)S(1)} %fusion.4), channel_id=1, replica_groups=mesh['tp'=4,'grp'=8] {'tp'}, use_global_device_ids=true, to_apply=%region_17.18 | all-reduce | flops 65536 | bytes 393216 | tf_op jit(solution)/shard_map/psum | solution.py:123
  551.2 4.0 all-to-all-start.3
  555.2 5.9 %all-to-all-done.3 = bf16[8,4,1024]{2,1,0:T(4,128)(2,1)S(1)} async-done(((bf16[8,4,1024]{2,1,0:T(4,128)(2,1)}), bf16[8,4,1024]{2,1,0:T(4,128)(2,1)S(1)}, u32[]{:S(2)}, u32[]{:S(2)}) %all-to-all-start.3) | async-done | bytes 65568 | tf_op jit(solution)/shard_map/all_to_all | solution.py:139
  (190 shorter events, 73.8 us)
Async XLA Ops:
  10.4 47.1 %all-to-all-start.4 = ((bf16[4,8,1024]{2,0,1:T(4,128)(2,1)}), bf16[4,8,1024]{2,0,1:T(4,128)(2,1)S(1)}, u32[]{:S(2)}, u32[]{:S(2)}) async-start(bf16[4,8,1024]{2,0,1:T(4,128)(2,1)} %get-tuple-element.60), calls=%async_computation.4 | async-start | bytes 131072 | tf_op jit(solution)/shard_map/all_to_all | solution.py:136
  31.0 12.1 %copy-start.5 = (bf16[2,4,3,2048]{3,1,2,0:T(4,128)(2,1)S(1)}, bf16[2,4,3,2048]{3,1,2,0:T(4,128)(2,1)}, u32[]{:S(2)}) copy-start(bf16[2,4,3,2048]{3,1,2,0:T(4,128)(2,1)} %param.16) | copy-start | bytes 294916
  31.1 12.2 %copy-start.8 = (f32[2,4,2048]{2,1,0:T(4,128)S(1)}, f32[2,4,2048]{2,1,0:T(4,128)}, u32[]{:S(2)}) copy-start(f32[2,4,2048]{2,1,0:T(4,128)} %param.23) | copy-start | bytes 196612
  31.1 12.2 %copy-start.9 = (f32[2,2048]{1,0:T(2,128)S(1)}, f32[2,2048]{1,0:T(2,128)}, u32[]{:S(2)}) copy-start(f32[2,2048]{1,0:T(2,128)} %param.24) | copy-start | bytes 49156
  31.1 12.3 %copy-start.19 = (f32[2,32]{1,0:T(2,128)S(1)}, f32[2,32]{1,0:T(2,128)}, u32[]{:S(2)}) copy-start(f32[2,32]{1,0:T(2,128)} %param.22) | copy-start | bytes 772
  44.1 92.2 %copy-start.6 = (f32[2048]{0:T(1024)}, f32[2048]{0:T(1024)S(1)}, u32[]{:S(2)}) copy-start(f32[2048]{0:T(1024)S(1)} %mul.533) | copy-start | bytes 24580
  44.1 12.2 %copy-start.22 = (u32[32]{0:T(128)S(1)}, u32[32]{0:T(128)}, u32[]{:S(2)}) copy-start(u32[32]{0:T(128)} %constant.77) | copy-start | bytes 388
  44.1 18.8 %copy-start.20 = (f32[2,32]{1,0:T(2,128)S(1)}, f32[2,32]{1,0:T(2,128)}, u32[]{:S(2)}) copy-start(f32[2,32]{1,0:T(2,128)} %param.21) | copy-start | bytes 772
  44.1 18.8 %copy-start.21 = (f32[2,32]{1,0:T(2,128)S(1)}, f32[2,32]{1,0:T(2,128)}, u32[]{:S(2)}) copy-start(f32[2,32]{1,0:T(2,128)} %param.20) | copy-start | bytes 772
  44.1 24.5 %copy-start.2 = (bf16[2,1024,384]{2,1,0:T(8,128)(2,1)S(1)}, bf16[2,1024,384]{2,1,0:T(8,128)(2,1)}, u32[]{:S(2)}) copy-start(bf16[2,1024,384]{2,1,0:T(8,128)(2,1)} %param.19) | copy-start | bytes 4718596
  57.5 11.0 %all-to-all-start = ((bf16[4,8,1024]{2,0,1:T(4,128)(2,1)}), bf16[4,8,1024]{2,0,1:T(4,128)(2,1)S(1)}, u32[]{:S(2)}, u32[]{:S(2)}) async-start(bf16[4,8,1024]{2,0,1:T(4,128)(2,1)} %get-tuple-element.59), calls=%async_computation | async-start | bytes 131072 | tf_op jit(solution)/shard_map/all_to_all | solution.py:136
  62.6 67.3 %all-reduce.13.cloned.1.call-start = ((), (), s32[]{:S(2)}) async-start(), calls=%async_computation.9 | async-start | bytes 1146880
  63.5 68.4 %copy-start.14 = (f32[32]{0:T(128)}, f32[32]{0:T(128)S(1)}, u32[]{:S(2)}) copy-start(f32[32]{0:T(128)S(1)} %get-tuple-element.70) | copy-start | bytes 388
  63.5 68.4 %copy-start.16 = (f32[32]{0:T(128)}, f32[32]{0:T(128)S(1)}, u32[]{:S(2)}) copy-start(f32[32]{0:T(128)S(1)} %get-tuple-element.73) | copy-start | bytes 388
  136.2 51.4 %copy-start.4 = (bf16[2,4,8192]{2,1,0:T(4,128)(2,1)S(1)}, bf16[2,4,8192]{2,1,0:T(4,128)(2,1)}, u32[]{:S(2)}) copy-start(bf16[2,4,8192]{2,1,0:T(4,128)(2,1)} %param.14) | copy-start | bytes 393220
  178.4 9.2 %all-to-all-start.1 = ((bf16[8,4,1024]{2,1,0:T(4,128)(2,1)}), bf16[8,4,1024]{2,1,0:T(4,128)(2,1)S(1)}, u32[]{:S(2)}, u32[]{:S(2)}) async-start(bf16[8,4,1024]{2,1,0:T(4,128)(2,1)} %constant_dynamic-update-slice_fusion), calls=%async_computation.1 | async-start | bytes 131072 | tf_op jit(solution)/shard_map/all_to_all | solution.py:139
  188.5 9.2 %all-to-all-start.2 = ((bf16[4,8,1024]{2,0,1:T(4,128)(2,1)}), bf16[4,8,1024]{2,0,1:T(4,128)(2,1)S(1)}, u32[]{:S(2)}, u32[]{:S(2)}) async-start(bf16[4,8,1024]{2,0,1:T(4,128)(2,1)} %multiply_convert_fusion.2), calls=%async_computation.2 | async-start | bytes 131072 | tf_op jit(solution)/shard_map/all_to_all | solution.py:136
  191.9 69.6 %all-reduce.17.cloned.1.call-start = ((), (), s32[]{:S(2)}) async-start(), calls=%async_computation.11 | async-start | bytes 2293760
  199.1 64.2 %copy-start.10 = (f32[32]{0:T(128)S(1)}, f32[32]{0:T(128)}, u32[]{:S(2)}) copy-start(f32[32]{0:T(128)} %get-tuple-element.69) | copy-start | bytes 388
  199.1 64.2 %copy-start.12 = (f32[32]{0:T(128)S(1)}, f32[32]{0:T(128)}, u32[]{:S(2)}) copy-start(f32[32]{0:T(128)} %get-tuple-element.74) | copy-start | bytes 388
  204.9 147.5 %all-gather.8.cloned.1.call-start = ((), (), s32[]{:S(2)}) async-start(), calls=%async_computation.8 | async-start | bytes 9437184 | tf_op jit(solution)/shard_map/all_gather | solution.py:74
  263.5 27.2 %copy-start.15 = (f32[32]{0:T(128)S(1)}, f32[32]{0:T(128)}, u32[]{:S(2)}) copy-start(f32[32]{0:T(128)} %copy-done.14) | copy-start | bytes 388
  263.5 27.2 %copy-start.17 = (f32[32]{0:T(128)S(1)}, f32[32]{0:T(128)}, u32[]{:S(2)}) copy-start(f32[32]{0:T(128)} %copy-done.16) | copy-start | bytes 388
  270.2 205.2 %all-reduce.15.cloned.1.call-start = ((), (), s32[]{:S(2)}) async-start(), calls=%async_computation.10 | async-start | bytes 1146880
  358.1 3.8 copy-start.7
  361.8 53.8 %copy-start.3 = (bf16[2,1024,384]{2,1,0:T(8,128)(2,1)S(1)}, bf16[2,1024,384]{2,1,0:T(8,128)(2,1)}, u32[]{:S(2)}) copy-start(bf16[2,1024,384]{2,1,0:T(8,128)(2,1)} %param.19) | copy-start | bytes 4718596
  415.8 6.0 %copy-start.18 = (f32[32]{0:T(128)S(1)}, f32[32]{0:T(128)}, u32[]{:S(2)}) copy-start(f32[32]{0:T(128)} %get-tuple-element.65) | copy-start | bytes 388
  415.9 61.4 %copy-start.11 = (f32[32]{0:T(128)S(1)}, f32[32]{0:T(128)}, u32[]{:S(2)}) copy-start(f32[32]{0:T(128)} %get-tuple-element.69) | copy-start | bytes 388
  415.9 61.4 %copy-start.13 = (f32[32]{0:T(128)S(1)}, f32[32]{0:T(128)}, u32[]{:S(2)}) copy-start(f32[32]{0:T(128)} %get-tuple-element.74) | copy-start | bytes 388
  415.9 61.6 %copy-start.1 = (bf16[4,32,64,128]{3,2,1,0:T(8,128)(2,1)S(1)}, bf16[4,32,64,128]{3,2,1,0:T(8,128)(2,1)}, u32[]{:S(2)}) copy-start(bf16[4,32,64,128]{3,2,1,0:T(8,128)(2,1)} %get-tuple-element.31) | copy-start | bytes 6291460
  542.0 9.2 %all-to-all-start.7 = ((bf16[8,4,1024]{2,1,0:T(4,128)(2,1)}), bf16[8,4,1024]{2,1,0:T(4,128)(2,1)S(1)}, u32[]{:S(2)}, u32[]{:S(2)}) async-start(bf16[8,4,1024]{2,1,0:T(4,128)(2,1)} %constant_dynamic-update-slice_fusion.24), calls=%async_computation.7 | async-start | bytes 131072 | tf_op jit(solution)/shard_map/all_to_all | solution.py:139
  551.2 9.9 %all-to-all-start.3 = ((bf16[8,4,1024]{2,1,0:T(4,128)(2,1)}), bf16[8,4,1024]{2,1,0:T(4,128)(2,1)S(1)}, u32[]{:S(2)}, u32[]{:S(2)}) async-start(bf16[8,4,1024]{2,1,0:T(4,128)(2,1)} %constant_dynamic-update-slice_fusion.8), calls=%async_computation.3 | async-start | bytes 131072 | tf_op jit(solution)/shard_map/all_to_all | solution.py:139
  (1 other events, 1.3 us)
Sparse Core Ops, SparseCore 0:
  74.7 55.1 all-reduce.12
  205.1 56.3 all-reduce.16
  270.4 82.0 all-gather.7
  422.0 53.4 all-reduce.14
